TPU v7x, 32 devices: a whole 2x2x4 slice. The times are simulated.
32 devices in a mesh: gx: 4 (over x, core), gy: 8 (over z, y).
Axes of the slice: x: 2, y: 2, z: 4, core: 2. Of those that a mesh axis runs over, the one named last changes fastest.
Arguments:
- activation: bfloat16 [32, 4096, 4096], P(None, 'gx', 'gy'), may hold values from -6 to 6
- cotangent: bfloat16 [32, 4096, 4096], P(None, 'gx', 'gy'), may hold values from -6 to 6
- point_weight: bfloat16 [32, 32], replicated, may hold values from -1 to 1
- spectral_weight: bfloat16 [2, 32, 32, 4096], P(None, None, None, ('gx', 'gy')), may hold values from -12 to 12
Outputs:
- grad_activation: bfloat16 [32, 4096, 4096], P(None, 'gx', 'gy')
- grad_point: float32 [32, 32], replicated
- grad_spectral: float32 [2, 32, 32, 4096], P(None, None, None, ('gx', 'gy'))
All inputs are finite; a program needn't handle non-finite values.
Results may differ from a plain program's by a relative error of at most 0.0065.
Values sent between devices are 32-bit elements; how exact they have to be, the bound alone decides.
A program may use at most 384 MiB of HBM per device.

v0:
```python
import math

import jax
import jax.numpy as jnp
from jax import lax
from jax.sharding import PartitionSpec as P

GRID_X = 4096
GRID_Y = 4096
MODES_X = 64
MODES_Y = 64


def twiddles(rows_here, cols_here):
    two_pi = 2.0 * math.pi
    row_start = lax.axis_index("gx") * rows_here
    col_start = lax.axis_index("gy") * cols_here
    freq_y = jnp.arange(MODES_Y, dtype=jnp.int32)
    col_ids = col_start + jnp.arange(cols_here, dtype=jnp.int32)
    phase_y = (col_ids[:, None] * freq_y[None, :] % GRID_Y).astype(jnp.float32) * (two_pi / GRID_Y)
    raw_x = jnp.arange(MODES_X, dtype=jnp.int32)
    freq_x = jnp.where(raw_x < MODES_X // 2, raw_x, raw_x + GRID_X - MODES_X)
    row_ids = row_start + jnp.arange(rows_here, dtype=jnp.int32)
    phase_x = (freq_x[:, None] * row_ids[None, :] % GRID_X).astype(jnp.float32) * (two_pi / GRID_X)
    return (jnp.cos(phase_y), jnp.sin(phase_y), jnp.cos(phase_x), jnp.sin(phase_x))


def forward_local(values, tables):
    cos_y, sin_y, cos_x, sin_x = tables
    channels, rows_here, cols_here = values.shape
    norm_scale = 1.0 / math.sqrt(GRID_X * GRID_Y)
    table_y = jnp.concatenate([cos_y, sin_y], axis=1)
    table_hi = table_y.astype(jnp.bfloat16)
    table_lo = (table_y - table_hi.astype(jnp.float32)).astype(jnp.bfloat16)
    flat_values = values.reshape(channels * rows_here, cols_here)
    along_y = jnp.dot(flat_values, table_hi, preferred_element_type=jnp.float32)
    along_y = along_y + jnp.dot(flat_values, table_lo, preferred_element_type=jnp.float32)
    along_y = along_y.reshape(channels, rows_here, 2 * MODES_Y)
    table_x = jnp.concatenate([cos_x, sin_x], axis=0)
    blocks = jnp.einsum(
        "kx,cxm->ckm",
        table_x,
        along_y,
        precision=lax.Precision.HIGH,
        preferred_element_type=jnp.float32,
    )
    real_part = blocks[:, :MODES_X, :MODES_Y] - blocks[:, MODES_X:, MODES_Y:]
    imag_part = -(blocks[:, MODES_X:, :MODES_Y] + blocks[:, :MODES_X, MODES_Y:])
    return jnp.stack([real_part, imag_part]).reshape(2, channels, MODES_X * MODES_Y) * norm_scale


def inverse_local(spectrum, tables):
    cos_y, sin_y, cos_x, sin_x = tables
    channels = spectrum.shape[1]
    rows_here = cos_x.shape[1]
    cols_here = cos_y.shape[0]
    norm_scale = 1.0 / math.sqrt(GRID_X * GRID_Y)
    real_part = spectrum[0].reshape(channels, MODES_X, MODES_Y)
    imag_part = spectrum[1].reshape(channels, MODES_X, MODES_Y)
    stacked = jnp.concatenate([real_part, imag_part], axis=1)
    left_real = jnp.concatenate([cos_x, -sin_x], axis=0)
    left_imag = jnp.concatenate([sin_x, cos_x], axis=0)
    sum_real = jnp.einsum(
        "kx,ckm->cxm",
        left_real,
        stacked,
        precision=lax.Precision.HIGH,
        preferred_element_type=jnp.float32,
    )
    sum_imag = jnp.einsum(
        "kx,ckm->cxm",
        left_imag,
        stacked,
        precision=lax.Precision.HIGH,
        preferred_element_type=jnp.float32,
    )
    joined = jnp.concatenate([sum_real, sum_imag], axis=2).reshape(
        channels * rows_here, 2 * MODES_Y
    )
    right_table = jnp.concatenate([cos_y.T, -sin_y.T], axis=0)
    synthesized = jnp.dot(
        joined, right_table, precision=lax.Precision.HIGH, preferred_element_type=jnp.float32
    )
    return (synthesized * norm_scale).reshape(channels, rows_here, cols_here)


def own_modes(partial_value):
    row_share = lax.psum_scatter(partial_value, "gx", scatter_dimension=2, tiled=True)
    return lax.psum_scatter(row_share, "gy", scatter_dimension=2, tiled=True)


def spread_modes(mode_share):
    return lax.all_gather(mode_share, ("gx", "gy"), axis=2, tiled=True)


def mix_modes(weight, spectrum):
    real_part = jnp.einsum("ocm,cm->om", weight[0], spectrum[0]) - jnp.einsum(
        "ocm,cm->om", weight[1], spectrum[1]
    )
    imag_part = jnp.einsum("ocm,cm->om", weight[0], spectrum[1]) + jnp.einsum(
        "ocm,cm->om", weight[1], spectrum[0]
    )
    return jnp.stack([real_part, imag_part])


def mix_adjoint(weight, spectrum):
    real_part = jnp.einsum("ocm,om->cm", weight[0], spectrum[0]) + jnp.einsum(
        "ocm,om->cm", weight[1], spectrum[1]
    )
    imag_part = jnp.einsum("ocm,om->cm", weight[0], spectrum[1]) - jnp.einsum(
        "ocm,om->cm", weight[1], spectrum[0]
    )
    return jnp.stack([real_part, imag_part])


def gelu_slope(values):
    cumulative = 0.5 * (1.0 + jax.scipy.special.erf(values * 0.7071067811865476))
    return cumulative + values * jnp.exp(-0.5 * values * values) * 0.3989422804014327


def per_device(activation, cotangent, point_weight, spectral_weight):
    channels, rows_here, cols_here = activation.shape
    norm_scale = 1.0 / math.sqrt(GRID_X * GRID_Y)
    tables = twiddles(rows_here, cols_here)
    weight_full = spectral_weight.astype(jnp.float32)
    forward_modes = own_modes(forward_local(activation, tables))
    spectral_part = inverse_local(spread_modes(mix_modes(weight_full, forward_modes)), tables)
    flat_act = activation.reshape(channels, rows_here * cols_here)
    pre = jnp.dot(point_weight, flat_act, preferred_element_type=jnp.float32)
    pre = pre + spectral_part.reshape(channels, rows_here * cols_here)
    slope = gelu_slope(pre)
    hidden = (
        cotangent.reshape(channels, rows_here * cols_here).astype(jnp.float32) * slope
    ).astype(jnp.bfloat16)
    local_grad = lax.dot_general(
        hidden, flat_act, (((1,), (1,)), ((), ())), preferred_element_type=jnp.float32
    )
    grad_point = lax.psum(local_grad, ("gx", "gy")) * norm_scale
    back_modes = own_modes(forward_local(hidden.reshape(channels, rows_here, cols_here), tables))
    grad_real = (
        back_modes[0][:, None, :] * forward_modes[0][None, :, :]
        + back_modes[1][:, None, :] * forward_modes[1][None, :, :]
    )
    grad_imag = (
        back_modes[1][:, None, :] * forward_modes[0][None, :, :]
        - back_modes[0][:, None, :] * forward_modes[1][None, :, :]
    )
    grad_spectral = jnp.stack([grad_real, grad_imag])
    back_field = inverse_local(spread_modes(mix_adjoint(weight_full, back_modes)), tables)
    grad_flat = jnp.dot(point_weight.T, hidden, preferred_element_type=jnp.float32)
    grad_flat = grad_flat + back_field.reshape(channels, rows_here * cols_here)
    grad_activation = grad_flat.astype(jnp.bfloat16).reshape(channels, rows_here, cols_here)
    return (grad_activation, grad_point, grad_spectral)


def solution(mesh):
    placed = (P(None, "gx", "gy"), P(None, "gx", "gy"), P(), P(None, None, None, ("gx", "gy")))
    return jax.shard_map(
        per_device,
        mesh=mesh,
        in_specs=placed,
        out_specs=(P(None, "gx", "gy"), P(), P(None, None, None, ("gx", "gy"))),
        check_vma=False,
    )
```

profile of v0, /device:TPU:0, one launch (start us, length us, event | category | flops | bytes accessed | tf_op | source)
XLA Modules:
  0.0 916.1 jit_solution(16001080461270312924)
XLA Ops:
  7.3 1.1 fusion.42
  8.5 22.8 %fusion.57 = f32[128,32768]{1,0:T(8,128)} fusion(bf16[32768,512]{1,0:T(8,128)(2,1)} %bitcast.133, f32[512,64]{1,0:T(8,128)S(1)} %get-tuple-element.39, f32[512,64]{1,0:T(8,128)S(1)} %get-tuple-element.38), kind=kOutput, calls=%fused_computation.122 | convolution fusion | flops 4295229440 | bytes 50593792 | tf_op jit(solution)/shard_map/dot_general | solution.py:36
  31.3 23.8 %convolution_add_fusion.1 = f32[128,32768]{1,0:T(8,128)} fusion(f32[128,32768]{1,0:T(8,128)} %fusion.57, bf16[512,128]{1,0:T(8,128)(2,1)S(1)} %subtract_convert_fusion, bf16[32768,512]{1,0:T(8,128)(2,1)} %bitcast.134), kind=kOutput, calls=%fused_computation.13 | convolution fusion | flops 4299161600 | bytes 67239936 | tf_op jit(solution)/shard_map/dot_general | solution.py:37
  55.1 15.7 %copy.78 = f32[16,8,32,1024]{3,2,1,0:T(8,128)S(1)} copy(f32[16,8,32,1024]{3,1,2,0:T(8,128)} %bitcast.142) | data formatting | bytes 33554432
  70.8 1.1 fusion.45
  72.0 6.9 fusion.23
  78.9 1.2 copy.81
  80.1 1.6 slice_subtract_fusion.1
  81.7 1.6 copy.10
  83.2 1.2 stack.41
  84.4 0.3 copy.11
  84.7 0.4 stack.42
  85.1 2.1 maximum_multiply_fusion
  87.3 27.6 %reduce-scatter.5.cloned.1.call-done = f32[2,32,1024]{2,1,0:T(8,128)} async-done(((f32[2,32,4096]{2,1,0:T(8,128)}), f32[2,32,1024]{2,1,0:T(8,128)}) %reduce-scatter.5.cloned.1.call-update) | async-done | bytes 262160 | tf_op jit(solution)/shard_map/reduce_scatter | solution.py:88
  115.0 65.7 %reduce-scatter.7.cloned.1.call-done = f32[2,32,128]{2,1,0:T(8,128)} async-done(((f32[2,32,1024]{2,1,0:T(8,128)}), f32[2,32,128]{2,1,0:T(8,128)}) %reduce-scatter.7.cloned.1.call-update) | async-done | bytes 32784 | tf_op jit(solution)/shard_map/reduce_scatter | solution.py:89
  180.7 1.3 slice_bitcast_fusion.7
  182.0 0.4 fusion.14
  182.4 0.6 pad_maximum_fusion.15
  183.1 31.4 %copy.77 = bf16[4,8,1024,512]{3,1,2,0:T(8,128)(2,1)} copy(bf16[4,8,1024,512]{3,2,1,0:T(8,128)(2,1)} %bitcast.135) | data formatting | bytes 67108864
  214.5 31.4 %copy.76 = f32[4,8,1024,512]{3,1,2,0:T(8,128)} copy(bf16[4,8,1024,512]{3,2,1,0:T(8,128)(2,1)} %bitcast.144) | data formatting | bytes 100663296
  246.0 1.2 fusion.46
  247.2 1.3 fusion.60
  248.5 0.4 reshape_squeeze.12
  248.9 0.3 copy.12
  249.3 1.4 reshape_squeeze.13
  250.6 1.6 copy.13
  252.2 3.7 convolution_bitcast_fusion.3
  255.9 3.7 convolution_bitcast_fusion.4
  259.6 6.4 pad_maximum_fusion
  265.9 17.4 %copy.14 = f32[32,1024,128]{2,1,0:T(8,128)} copy(f32[32,1024,128]{1,2,0:T(8,128)} %pad_maximum_fusion) | data formatting | bytes 33554432 | tf_op jit(solution)/shard_map/concatenate | solution.py:77
  283.4 37.4 %convolution_multiply_fusion.1 = f32[32768,512]{1,0:T(8,128)} fusion(f32[32768,128]{1,0:T(8,128)} %bitcast.140, f32[64,512]{1,0:T(8,128)S(1)} %copy-done.17, f32[64,512]{1,0:T(8,128)S(1)} %get-tuple-element.36), kind=kOutput, calls=%fused_computation.12 | convolution fusion | flops 12901744640 | bytes 84148224 | tf_op jit(solution)/shard_map/dot_general | solution.py:81
  320.8 58.2 %reshape_reshape.9 = f32[32,524288]{1,0:T(8,128)} reshape(f32[32768,512]{1,0:T(8,128)} %convolution_multiply_fusion.1) | data formatting | bytes 134217728 | tf_op jit(solution)/shard_map/reshape;reshape | solution.py:130
  378.9 66.0 %fusion.7 = bf16[32,524288]{1,0:T(8,128)(2,1)} fusion(f32[32,524288]{1,0:T(8,128)} %bitcast.66, f32[32,524288]{1,0:T(8,128)} %reshape_reshape.9, bf16[32,32]{1,0:T(8,128)(2,1)S(1)} %copy-done, bf16[32,524288]{1,0:T(8,128)(2,1)} %bitcast.136), kind=kOutput, calls=%fused_computation.10 | convolution fusion | flops 1258291200 | bytes 201328640 | tf_op jit(solution)/shard_map/dot_general | solution.py:129
  445.0 41.6 %reshape_reshape.10 = bf16[32768,512]{1,0:T(8,128)(2,1)} reshape(bf16[32,524288]{1,0:T(8,128)(2,1)} %fusion.7) | data formatting | bytes 67108864 | tf_op jit(solution)/shard_map/reshape;reshape | solution.py:35
  486.6 18.6 %fusion.55 = f32[32768,128]{1,0:T(8,128)} fusion(bf16[32768,512]{1,0:T(8,128)(2,1)} %reshape_reshape.10, f32[512,64]{1,0:T(8,128)S(1)} %copy-done.8, f32[512,64]{1,0:T(8,128)S(1)} %copy-done.6), kind=kOutput, calls=%fused_computation.121 | convolution fusion | flops 4295229440 | bytes 50593792 | tf_op jit(solution)/shard_map/dot_general | solution.py:36
  505.1 25.0 %convolution_add_fusion.2 = f32[32768,128]{1,0:T(8,128)} fusion(f32[32768,128]{1,0:T(8,128)} %fusion.55, bf16[32768,512]{1,0:T(8,128)(2,1)} %reshape_reshape.10, bf16[512,128]{1,0:T(8,128)(2,1)S(1)} %copy-done.14), kind=kOutput, calls=%fused_computation.14 | convolution fusion | flops 4299161600 | bytes 67239936 | tf_op jit(solution)/shard_map/dot_general | solution.py:37
  530.1 17.5 %convolution_bitcast_fusion.5 = f32[32,128,128]{1,2,0:T(8,128)S(1)} fusion(f32[32,1024,128]{2,1,0:T(8,128)} %bitcast.141, f32[64,1024]{1,0:T(8,128)S(1)} %copy-done.2, f32[64,1024]{1,0:T(8,128)S(1)} %copy-done.4), kind=kOutput, calls=%fused_computation.22 | convolution fusion | flops 3221356544 | bytes 19398656 | tf_op jit(solution)/shard_map/kx,cxm->ckm/dot_general | solution.py:40
  547.6 1.6 slice_subtract_fusion
  549.2 1.6 copy.16
  550.8 1.2 stack.47
  551.9 0.3 copy.17
  552.3 0.4 stack.48
  552.6 2.1 maximum_multiply_fusion.1
  554.8 23.9 %reduce-scatter.9.cloned.1.call-done = f32[2,32,1024]{2,1,0:T(8,128)} async-done(((f32[2,32,4096]{2,1,0:T(8,128)}), f32[2,32,1024]{2,1,0:T(8,128)}) %reduce-scatter.9.cloned.1.call-update) | async-done | bytes 262160 | tf_op jit(solution)/shard_map/reduce_scatter | solution.py:88
  578.8 65.5 %reduce-scatter.11.cloned.1.call-done = f32[2,32,128]{2,1,0:T(8,128)} async-done(((f32[2,32,1024]{2,1,0:T(8,128)}), f32[2,32,128]{2,1,0:T(8,128)}) %reduce-scatter.11.cloned.1.call-update) | async-done | bytes 32784 | tf_op jit(solution)/shard_map/reduce_scatter | solution.py:89
  644.3 0.7 slice_bitcast_fusion.3
  645.3 0.6 pad_maximum_fusion.16
  646.0 22.7 %fusion.61 = f32[32,32]{1,0:T(8,128)S(1)} fusion(bf16[32,524288]{1,0:T(8,128)(2,1)} %fusion.7, bf16[32,524288]{1,0:T(8,128)(2,1)} %bitcast.137), kind=kOutput, calls=%fused_computation.125 | convolution fusion | flops 1073741824 | bytes 67112960 | tf_op jit(solution)/shard_map/dot_general | solution.py:135
  668.7 40.5 %psum.7 = f32[32,32]{1,0:T(8,128)S(1)} all-reduce(f32[32,32]{1,0:T(8,128)S(1)} %fusion.61), channel_id=1, replica_groups=mesh['gx'=4,'gy'=8] {'gx','gy'}, use_global_device_ids=true, to_apply=%region_4.5 | all-reduce | flops 1024 | bytes 8192 | tf_op jit(solution)/shard_map/psum | solution.py:138
  709.1 0.6 broadcast_multiply_fusion
  709.9 1.0 pad_maximum_fusion.4
  710.9 1.3 fusion.59
  712.2 0.4 reshape_squeeze.14
  712.6 0.3 copy.18
  713.0 1.4 reshape_squeeze.15
  714.4 1.6 copy.19
  715.9 3.7 convolution_bitcast_fusion.1
  719.6 3.7 convolution_bitcast_fusion.2
  723.3 6.5 pad_maximum_fusion.1
  729.8 17.4 %copy.20 = f32[32,1024,128]{2,1,0:T(8,128)} copy(f32[32,1024,128]{1,2,0:T(8,128)} %pad_maximum_fusion.1) | data formatting | bytes 33554432 | tf_op jit(solution)/shard_map/concatenate | solution.py:77
  747.2 37.2 %convolution_multiply_fusion = f32[32768,512]{1,0:T(8,128)} fusion(f32[32768,128]{1,0:T(8,128)} %bitcast.139, f32[64,512]{1,0:T(8,128)S(1)} %copy-done.18, f32[64,512]{1,0:T(8,128)S(1)} %copy-done.16), kind=kOutput, calls=%fused_computation.11 | convolution fusion | flops 12901744640 | bytes 84148224 | tf_op jit(solution)/shard_map/dot_general | solution.py:81
  784.4 58.1 %reshape_reshape.11 = f32[32,524288]{1,0:T(8,128)} reshape(f32[32768,512]{1,0:T(8,128)} %convolution_multiply_fusion) | data formatting | bytes 134217728 | tf_op jit(solution)/shard_map/reshape;reshape | solution.py:151
  842.5 43.8 %fusion.1 = bf16[32,524288]{1,0:T(8,128)(2,1)} fusion(f32[32,524288]{1,0:T(8,128)} %reshape_reshape.11, bf16[32,524288]{1,0:T(8,128)(2,1)} %fusion.7, bf16[32,32]{1,0:T(8,128)(2,1)S(1)} %copy-done), kind=kOutput, calls=%fused_computation.3 | convolution fusion | flops 1107296256 | bytes 134219776 | tf_op jit(solution)/shard_map/dot_general | solution.py:150
  886.3 22.7 %copy.79 = bf16[4,8,1024,512]{3,2,1,0:T(8,128)(2,1)} copy(bf16[4,8,1024,512]{3,1,2,0:T(8,128)(2,1)} %bitcast.138) | data formatting | bytes 67108864
  (65 shorter events, 0.9 us)
Async XLA Ops:
  7.2 371.8 %copy-start = (bf16[32,32]{1,0:T(8,128)(2,1)S(1)}, bf16[32,32]{1,0:T(8,128)(2,1)}, u32[]{:S(2)}) copy-start(bf16[32,32]{1,0:T(8,128)(2,1)} %param.6) | copy-start | bytes 6148
  7.2 107.7 %reduce-scatter.5.cloned.1.call-start = ((), (), s32[]{:S(2)}) async-start(), calls=%async_computation.4 | async-start | bytes 1310720 | tf_op jit(solution)/shard_map/reduce_scatter | solution.py:88
  8.4 46.7 %copy-start.5 = (f32[512,64]{1,0:T(8,128)}, f32[512,64]{1,0:T(8,128)S(1)}, u32[]{:S(2)}) copy-start(f32[512,64]{1,0:T(8,128)S(1)} %get-tuple-element.38) | copy-start | bytes 393220
  8.4 46.7 %copy-start.7 = (f32[512,64]{1,0:T(8,128)}, f32[512,64]{1,0:T(8,128)S(1)}, u32[]{:S(2)}) copy-start(f32[512,64]{1,0:T(8,128)S(1)} %get-tuple-element.39) | copy-start | bytes 393220
  8.5 46.6 %copy-start.13 = (bf16[512,128]{1,0:T(8,128)(2,1)}, bf16[512,128]{1,0:T(8,128)(2,1)S(1)}, u32[]{:S(2)}) copy-start(bf16[512,128]{1,0:T(8,128)(2,1)S(1)} %subtract_convert_fusion) | copy-start | bytes 393220
  55.1 126.9 %copy-start.11 = (bf16[2,32,32,128]{3,2,1,0:T(8,128)(2,1)S(1)}, bf16[2,32,32,128]{3,2,1,0:T(8,128)(2,1)}, u32[]{:S(2)}) copy-start(bf16[2,32,32,128]{3,2,1,0:T(8,128)(2,1)} %param.7) | copy-start | bytes 1572868
  71.9 180.3 %copy-start.3 = (f32[64,1024]{1,0:T(8,128)}, f32[64,1024]{1,0:T(8,128)S(1)}, u32[]{:S(2)}) copy-start(f32[64,1024]{1,0:T(8,128)S(1)} %get-tuple-element.34) | copy-start | bytes 786436
  71.9 183.9 %copy-start.1 = (f32[64,1024]{1,0:T(8,128)}, f32[64,1024]{1,0:T(8,128)S(1)}, u32[]{:S(2)}) copy-start(f32[64,1024]{1,0:T(8,128)S(1)} %get-tuple-element.35) | copy-start | bytes 786436
  72.0 183.9 %copy-start.9 = (f32[64,1024]{1,0:T(8,128)}, f32[64,1024]{1,0:T(8,128)S(1)}, u32[]{:S(2)}) copy-start(f32[64,1024]{1,0:T(8,128)S(1)} %get-tuple-element.33) | copy-start | bytes 786436
  87.2 93.4 %reduce-scatter.7.cloned.1.call-start = ((), (), s32[]{:S(2)}) async-start(), calls=%async_computation.5 | async-start | bytes 294912 | tf_op jit(solution)/shard_map/reduce_scatter | solution.py:89
  114.9 132.2 %all-gather.3.cloned.1.call-start = ((), (), s32[]{:S(2)}) async-start(), calls=%async_computation.6 | async-start | bytes 1081344 | tf_op jit(solution)/shard_map/all_gather | solution.py:93
  183.1 395.6 %reduce-scatter.9.cloned.1.call-start = ((), (), s32[]{:S(2)}) async-start(), calls=%async_computation.7 | async-start | bytes 1310720 | tf_op jit(solution)/shard_map/reduce_scatter | solution.py:88
  247.2 36.2 %copy-start.15 = (f32[64,512]{1,0:T(8,128)}, f32[64,512]{1,0:T(8,128)S(1)}, u32[]{:S(2)}) copy-start(f32[64,512]{1,0:T(8,128)S(1)} %get-tuple-element.36) | copy-start | bytes 393220
  259.6 23.8 %copy-start.17 = (f32[64,512]{1,0:T(8,128)S(1)}, f32[64,512]{1,0:T(8,128)}, u32[]{:S(2)}) copy-start(f32[64,512]{1,0:T(8,128)} %get-tuple-element.37) | copy-start | bytes 393220
  444.9 41.6 %copy-start.6 = (f32[512,64]{1,0:T(8,128)S(1)}, f32[512,64]{1,0:T(8,128)}, u32[]{:S(2)}) copy-start(f32[512,64]{1,0:T(8,128)} %copy-done.5) | copy-start | bytes 393220
  445.0 41.6 %copy-start.8 = (f32[512,64]{1,0:T(8,128)S(1)}, f32[512,64]{1,0:T(8,128)}, u32[]{:S(2)}) copy-start(f32[512,64]{1,0:T(8,128)} %copy-done.7) | copy-start | bytes 393220
  486.6 18.6 %copy-start.14 = (bf16[512,128]{1,0:T(8,128)(2,1)S(1)}, bf16[512,128]{1,0:T(8,128)(2,1)}, u32[]{:S(2)}) copy-start(bf16[512,128]{1,0:T(8,128)(2,1)} %copy-done.13) | copy-start | bytes 393220
  505.1 25.0 %copy-start.2 = (f32[64,1024]{1,0:T(8,128)S(1)}, f32[64,1024]{1,0:T(8,128)}, u32[]{:S(2)}) copy-start(f32[64,1024]{1,0:T(8,128)} %copy-done.1) | copy-start | bytes 786436
  505.1 25.0 %copy-start.4 = (f32[64,1024]{1,0:T(8,128)S(1)}, f32[64,1024]{1,0:T(8,128)}, u32[]{:S(2)}) copy-start(f32[64,1024]{1,0:T(8,128)} %copy-done.3) | copy-start | bytes 786436
  530.1 115.0 %copy-start.12 = (bf16[2,32,32,128]{3,2,1,0:T(8,128)(2,1)S(1)}, bf16[2,32,32,128]{3,2,1,0:T(8,128)(2,1)}, u32[]{:S(2)}) copy-start(bf16[2,32,32,128]{3,2,1,0:T(8,128)(2,1)} %param.7) | copy-start | bytes 1572868
  554.8 89.6 %reduce-scatter.11.cloned.1.call-start = ((), (), s32[]{:S(2)}) async-start(), calls=%async_computation.8 | async-start | bytes 294912 | tf_op jit(solution)/shard_map/reduce_scatter | solution.py:89
  578.8 132.2 %all-gather.5.cloned.1.call-start = ((), (), s32[]{:S(2)}) async-start(), calls=%async_computation.9 | async-start | bytes 1081344 | tf_op jit(solution)/shard_map/all_gather | solution.py:93
  645.9 63.8 %copy-start.19 = (f32[32,128]{1,0:T(8,128)S(1)}, f32[32,128]{1,0:T(8,128)}, u32[]{:S(2)}) copy-start(f32[32,128]{1,0:T(8,128)} %get-tuple-element.29) | copy-start | bytes 49156
  645.9 63.8 %copy-start.20 = (f32[32,128]{1,0:T(8,128)S(1)}, f32[32,128]{1,0:T(8,128)}, u32[]{:S(2)}) copy-start(f32[32,128]{1,0:T(8,128)} %get-tuple-element.32) | copy-start | bytes 49156
  645.9 73.7 %copy-start.10 = (f32[64,1024]{1,0:T(8,128)S(1)}, f32[64,1024]{1,0:T(8,128)}, u32[]{:S(2)}) copy-start(f32[64,1024]{1,0:T(8,128)} %copy-done.9) | copy-start | bytes 786436
  723.3 23.9 %copy-start.16 = (f32[64,512]{1,0:T(8,128)S(1)}, f32[64,512]{1,0:T(8,128)}, u32[]{:S(2)}) copy-start(f32[64,512]{1,0:T(8,128)} %copy-done.15) | copy-start | bytes 393220
  723.3 23.9 %copy-start.18 = (f32[64,512]{1,0:T(8,128)S(1)}, f32[64,512]{1,0:T(8,128)}, u32[]{:S(2)}) copy-start(f32[64,512]{1,0:T(8,128)} %get-tuple-element.37) | copy-start | bytes 393220
Sparse Core Ops, SparseCore 0:
  87.4 27.4 reduce-scatter.4
  118.2 62.4 reduce-scatter.6
  184.2 51.3 all-gather.2
  554.9 23.7 reduce-scatter.8
  581.9 62.3 reduce-scatter.10
  647.1 51.7 all-gather.4
where the time goes:
time: 925 us; the launch traced here: 916 us
  matrix products  336 us (36%)
  local copies, waits for them, and re-layouts  314 us (34%)
  waiting for transfers between devices  183 us (20%)
  blocking collectives  40.5 us (4%)
  other arithmetic  27.4 us (3%)
  between operations  14.8 us (2%)
    reduce_scatter x2, waiting for transfers between devices, own_modes(): return lax.psum_scatter(row_share, 'gy', scatter_dimension=2, tiled=True)  131 us
    unnamed x46, local copies, waits for them, and re-layouts  101 us
    dot_general x2, matrix products, inverse_local(): jnp.dot(joined, right_table, precision=lax.Precision.HIGH, preferred_elem...  74.6 us
    dot_general x1, matrix products, per_device(): pre = jnp.dot(point_weight, flat_act, preferred_element_type=jnp.float32)  66 us
    another operation x1, local copies, waits for them, and re-layouts, per_device(): pre = pre + spectral_part.reshape(channels, rows_here * cols_here)  58.2 us
    another operation x1, local copies, waits for them, and re-layouts, per_device(): grad_flat = grad_flat + back_field.reshape(channels, rows_here * cols_here)  58.1 us
    reduce_scatter x2, waiting for transfers between devices, own_modes(): lax.psum_scatter(partial_value, 'gx', scatter_dimension=2, tiled=True)  51.5 us
    dot_general x2, matrix products, forward_local(): jnp.dot(flat_values, table_lo, preferred_element_type=jnp.float32)  48.7 us
  transfers between devices with their start and end apart: 6, of which 4 were waited for; matrix products, arithmetic and copies ran while one was open for 10% of the time, Pallas kernels for 0%

commit v1 on v0

v1 whole, which is shorter than its diff:
```python
import functools
import math

import jax
import jax.numpy as jnp
from jax import lax
from jax.experimental import pallas as pl
from jax.experimental.pallas import tpu as pltpu
from jax.sharding import PartitionSpec as P

GRID_X = 4096
GRID_Y = 4096
MODES_X = 64
MODES_Y = 64


def twiddles(rows_here, cols_here):
    two_pi = 2.0 * math.pi
    row_start = lax.axis_index("gx") * rows_here
    col_start = lax.axis_index("gy") * cols_here
    freq_y = jnp.arange(MODES_Y, dtype=jnp.int32)
    col_ids = col_start + jnp.arange(cols_here, dtype=jnp.int32)
    phase_y = (col_ids[:, None] * freq_y[None, :] % GRID_Y).astype(jnp.float32) * (two_pi / GRID_Y)
    raw_x = jnp.arange(MODES_X, dtype=jnp.int32)
    freq_x = jnp.where(raw_x < MODES_X // 2, raw_x, raw_x + GRID_X - MODES_X)
    row_ids = row_start + jnp.arange(rows_here, dtype=jnp.int32)
    phase_x = (freq_x[:, None] * row_ids[None, :] % GRID_X).astype(jnp.float32) * (two_pi / GRID_X)
    return (jnp.cos(phase_y), jnp.sin(phase_y), jnp.cos(phase_x), jnp.sin(phase_x))


def mix_modes(weight, spectrum):
    real_part = jnp.einsum("ocm,cm->om", weight[0], spectrum[0]) - jnp.einsum(
        "ocm,cm->om", weight[1], spectrum[1]
    )
    imag_part = jnp.einsum("ocm,cm->om", weight[0], spectrum[1]) + jnp.einsum(
        "ocm,cm->om", weight[1], spectrum[0]
    )
    return jnp.stack([real_part, imag_part])


def mix_adjoint(weight, spectrum):
    real_part = jnp.einsum("ocm,om->cm", weight[0], spectrum[0]) + jnp.einsum(
        "ocm,om->cm", weight[1], spectrum[1]
    )
    imag_part = jnp.einsum("ocm,om->cm", weight[0], spectrum[1]) - jnp.einsum(
        "ocm,om->cm", weight[1], spectrum[0]
    )
    return jnp.stack([real_part, imag_part])


def gelu_slope(values):
    cumulative = 0.5 * (1.0 + jax.scipy.special.erf(values * 0.7071067811865476))
    return cumulative + values * jnp.exp(-0.5 * values * values) * 0.3989422804014327


SUB = 16


def split(table):
    high = table.astype(jnp.bfloat16)
    return high, (table - high.astype(jnp.float32)).astype(jnp.bfloat16)


def forward_kernel(values_ref, table_y_ref, table_x_ref, out_ref):
    both = jnp.dot(values_ref[0], table_y_ref[...], preferred_element_type=jnp.float32)
    width = 2 * MODES_Y
    along = both[:, :width] + both[:, width:]
    high = along.astype(jnp.bfloat16)
    low = (along - high.astype(jnp.float32)).astype(jnp.bfloat16)
    joined = jnp.concatenate([high, low], axis=1)
    parts = jnp.dot(table_x_ref[...], joined, preferred_element_type=jnp.float32)
    parts = parts[:, :width] + parts[:, width:]
    parts = parts[: 2 * MODES_X] + parts[2 * MODES_X :]
    upper = parts[:MODES_X]
    lower = pltpu.roll(parts[MODES_X:], MODES_Y, 1)
    lane = lax.broadcasted_iota(jnp.int32, upper.shape, 1)
    out_ref[0] = jnp.where(lane < MODES_Y, upper - lower, -(upper + lower))


def forward_local(values, table_y, table_x):
    channels, rows, cols = values.shape
    norm_scale = 1.0 / math.sqrt(GRID_X * GRID_Y)
    out = pl.pallas_call(
        forward_kernel,
        grid=(channels,),
        out_shape=jax.ShapeDtypeStruct((channels, MODES_X, 2 * MODES_Y), jnp.float32),
        in_specs=[
            pl.BlockSpec((1, rows, cols), lambda c: (c, 0, 0)),
            pl.BlockSpec(table_y.shape, lambda c: (0, 0)),
            pl.BlockSpec(table_x.shape, lambda c: (0, 0)),
        ],
        out_specs=pl.BlockSpec((1, MODES_X, 2 * MODES_Y), lambda c: (c, 0, 0)),
        name="forward_modes",
    )(values, table_y, table_x)
    out = out.reshape(channels, MODES_X, 2, MODES_Y).transpose(2, 0, 1, 3) * norm_scale
    return out.reshape(2 * channels, MODES_X * MODES_Y)


def rows_kernel(modes_ref, table_ref, out_ref):
    modes = modes_ref[0].astype(jnp.bfloat16)
    value = jnp.dot(
        table_ref[...], jnp.concatenate([modes, modes], axis=0), preferred_element_type=jnp.float32
    )
    out_ref[0] = value.astype(jnp.bfloat16)


def rows_of(spectrum, table):
    channels = spectrum.shape[1]
    norm_scale = 1.0 / math.sqrt(GRID_X * GRID_Y)
    real = spectrum[0].reshape(channels, MODES_X, MODES_Y) * norm_scale
    imag = spectrum[1].reshape(channels, MODES_X, MODES_Y) * norm_scale
    modes = jnp.concatenate(
        [jnp.concatenate([real, imag], axis=2), jnp.concatenate([-imag, real], axis=2)], axis=1
    )
    rows = table.shape[0]
    return pl.pallas_call(
        rows_kernel,
        grid=(channels,),
        out_shape=jax.ShapeDtypeStruct((channels, rows, 2 * MODES_Y), jnp.bfloat16),
        in_specs=[
            pl.BlockSpec((1, 2 * MODES_X, 2 * MODES_Y), lambda c: (c, 0, 0)),
            pl.BlockSpec(table.shape, lambda c: (0, 0)),
        ],
        out_specs=pl.BlockSpec((1, rows, 2 * MODES_Y), lambda c: (c, 0, 0)),
        name="synthesis_rows",
    )(modes, table)


def field_block(mix_ref, flat, rows_ref, table_ref):
    rows = rows_ref[...].reshape(flat.shape[0], 2 * MODES_Y)
    value = jnp.dot(mix_ref[...], flat, preferred_element_type=jnp.float32)
    return value + jnp.dot(
        jnp.concatenate([rows, rows], axis=1), table_ref[...], preferred_element_type=jnp.float32
    )


def hidden_kernel(act_ref, cot_ref, rows_ref, mix_ref, table_ref, hidden_ref, point_ref, total):
    step = pl.program_id(0)
    channels, sub, cols = act_ref.shape
    size = channels * sub

    @pl.when(step == 0)
    def _():
        total[...] = jnp.zeros_like(total)

    flat = act_ref[...].reshape(size, cols)
    pre = field_block(mix_ref, flat, rows_ref, table_ref)
    slope = gelu_slope(pre)
    cot = cot_ref[...].reshape(size, cols).astype(jnp.float32)
    hidden = (cot * slope).astype(jnp.bfloat16)
    hidden_ref[...] = hidden.reshape(channels, sub, cols)
    total[...] += lax.dot_general(
        hidden, flat, (((1,), (1,)), ((), ())), preferred_element_type=jnp.float32
    )

    @pl.when(step == pl.num_programs(0) - 1)
    def _():
        row = lax.broadcasted_iota(jnp.int32, (size, size), 0)
        col = lax.broadcasted_iota(jnp.int32, (size, size), 1)
        kept = jnp.where(row % sub == col % sub, total[...], 0.0)
        pick_row = lax.broadcasted_iota(jnp.int32, (channels, size), 0)
        pick_col = lax.broadcasted_iota(jnp.int32, (channels, size), 1)
        pick = jnp.where(pick_col // sub == pick_row, 1.0, 0.0)
        half = jnp.dot(
            pick, kept, precision=lax.Precision.HIGHEST, preferred_element_type=jnp.float32
        )
        point_ref[...] = lax.dot_general(
            half,
            pick,
            (((1,), (1,)), ((), ())),
            precision=lax.Precision.HIGHEST,
            preferred_element_type=jnp.float32,
        )


def grad_kernel(hidden_ref, rows_ref, mix_ref, table_ref, out_ref):
    channels, sub, cols = hidden_ref.shape
    flat = hidden_ref[...].reshape(channels * sub, cols)
    value = field_block(mix_ref, flat, rows_ref, table_ref)
    out_ref[...] = value.astype(jnp.bfloat16).reshape(channels, sub, cols)


def block_of(width):
    return lambda channels: pl.BlockSpec((channels, SUB, width), lambda i: (0, i, 0))


def whole(array):
    return pl.BlockSpec(array.shape, lambda i: (0, 0))


def hidden_of(activation, cotangent, rows, mix, table):
    channels, rows_here, cols = activation.shape
    wide = block_of(cols)(channels)
    size = channels * SUB
    return pl.pallas_call(
        hidden_kernel,
        grid=(rows_here // SUB,),
        out_shape=(
            jax.ShapeDtypeStruct(activation.shape, jnp.bfloat16),
            jax.ShapeDtypeStruct((channels, channels), jnp.float32),
        ),
        in_specs=[wide, wide, block_of(2 * MODES_Y)(channels), whole(mix), whole(table)],
        out_specs=(wide, pl.BlockSpec((channels, channels), lambda i: (0, 0))),
        scratch_shapes=[pltpu.VMEM((size, size), jnp.float32)],
        name="hidden",
    )(activation, cotangent, rows, mix, table)


def grad_of(hidden, rows, mix, table):
    channels, rows_here, cols = hidden.shape
    wide = block_of(cols)(channels)
    return pl.pallas_call(
        grad_kernel,
        grid=(rows_here // SUB,),
        out_shape=jax.ShapeDtypeStruct(hidden.shape, jnp.bfloat16),
        in_specs=[wide, block_of(2 * MODES_Y)(channels), whole(mix), whole(table)],
        out_specs=wide,
        name="grad",
    )(hidden, rows, mix, table)


def own_sums(partial_value, devices):
    lines, modes = partial_value.shape
    chunks = partial_value.reshape(lines, devices, modes // devices).transpose(1, 0, 2)
    moved = lax.all_to_all(chunks, ("gx", "gy"), split_axis=0, concat_axis=0, tiled=True)
    return jnp.sum(moved, axis=0)


def spread(share):
    return lax.all_gather(share, ("gx", "gy"), axis=1, tiled=True)


def per_device(devices, activation, cotangent, point_weight, spectral_weight):
    channels, rows_here, cols_here = activation.shape
    norm_scale = 1.0 / math.sqrt(GRID_X * GRID_Y)
    cos_y, sin_y, cos_x, sin_x = twiddles(rows_here, cols_here)
    fwd_y = jnp.concatenate(split(jnp.concatenate([cos_y, sin_y], axis=1)), axis=1)
    fwd_x = jnp.concatenate(split(jnp.concatenate([cos_x, sin_x], axis=0)), axis=0)
    inv_x = jnp.concatenate(split(jnp.concatenate([cos_x.T, sin_x.T], axis=1)), axis=1)
    inv_y = jnp.concatenate(split(jnp.concatenate([cos_y.T, -sin_y.T], axis=0)), axis=0)
    eye = jnp.eye(SUB, dtype=jnp.bfloat16)
    mix_point = jnp.kron(point_weight, eye)
    mix_back = jnp.kron(point_weight.T, eye)
    weight_full = spectral_weight.astype(jnp.float32)
    mode_count = MODES_X * MODES_Y
    share = mode_count // devices

    forward_modes = own_sums(forward_local(activation, fwd_y, fwd_x), devices)
    forward_modes = forward_modes.reshape(2, channels, share)
    mixed = mix_modes(weight_full, forward_modes).reshape(2 * channels, share)
    rows = rows_of(spread(mixed).reshape(2, channels, mode_count), inv_x)
    hidden, local_grad = hidden_of(activation, cotangent, rows, mix_point, inv_y)

    back_partial = forward_local(hidden, fwd_y, fwd_x)
    each = channels * channels // devices
    point_lines = jnp.pad(local_grad.reshape(devices, each), ((0, 0), (0, share - each)))
    sums = own_sums(
        jnp.concatenate([back_partial, point_lines.reshape(1, mode_count)], axis=0), devices
    )
    back_modes = sums[: 2 * channels].reshape(2, channels, share)
    grad_real = (
        back_modes[0][:, None, :] * forward_modes[0][None, :, :]
        + back_modes[1][:, None, :] * forward_modes[1][None, :, :]
    )
    grad_imag = (
        back_modes[1][:, None, :] * forward_modes[0][None, :, :]
        - back_modes[0][:, None, :] * forward_modes[1][None, :, :]
    )
    grad_spectral = jnp.stack([grad_real, grad_imag])
    adjoint = mix_adjoint(weight_full, back_modes).reshape(2 * channels, share)
    gathered = spread(jnp.concatenate([adjoint, sums[2 * channels :]], axis=0))
    grad_point = gathered[2 * channels].reshape(devices, share)[:, :each]
    grad_point = grad_point.reshape(channels, channels) * norm_scale
    back_rows = rows_of(gathered[: 2 * channels].reshape(2, channels, mode_count), inv_x)
    grad_activation = grad_of(hidden, back_rows, mix_back, inv_y)
    return (grad_activation, grad_point, grad_spectral)


def solution(mesh):
    placed = (P(None, "gx", "gy"), P(None, "gx", "gy"), P(), P(None, None, None, ("gx", "gy")))
    return jax.shard_map(
        functools.partial(per_device, mesh.shape["gx"] * mesh.shape["gy"]),
        mesh=mesh,
        in_specs=placed,
        out_specs=(P(None, "gx", "gy"), P(), P(None, None, None, ("gx", "gy"))),
        check_vma=False,
    )
```

time: 925 us -> 489 us (0.53)
  matrix products: 336 us -> 0 us
  local copies, waits for them, and re-layouts: 314 us -> 32.7 us
  Pallas kernels: 0 us -> 262 us
  waiting for transfers between devices: 183 us -> 74.3 us
  blocking collectives: 40.5 us -> 69 us
    dot_general x15 -> x0, matrix products: 336 us -> none  [the longest x2 74.6 us: inverse_local(): jnp.dot(joined, right_table, precision=lax.Precision.HIGH, preferred_elem...]
    pallas_call x0 -> x6, Pallas kernels: none -> 262 us  [the longest x1 86.2 us: hidden_of(): pl.pallas_call(hidden_kernel, grid=(rows_here // SUB,), out_shape=(jax.Sh...]
    reduce_scatter x4 -> x0, waiting for transfers between devices: 183 us -> none  [the longest x2 131 us: own_modes(): return lax.psum_scatter(row_share, 'gy', scatter_dimension=2, tiled=True)]
    another operation x15 -> x1, local copies, waits for them, and re-layouts: 168 us -> 1.8 us  [own_sums(): partial_value.reshape(lines, devices, modes // devices).transpose(1, 0, 2)]
    unnamed x46 -> x6, local copies, waits for them, and re-layouts: 101 us -> 0.02 us
    all_gather x2, waiting for transfers between devices: 0.01 us -> 74.2 us  [spread(): return lax.all_gather(share, ('gx', 'gy'), axis=1, tiled=True)]
    all_to_all x0 -> x2, blocking collectives: none -> 69 us  [own_sums(): lax.all_to_all(chunks, ('gx', 'gy'), split_axis=0, concat_axis=0, tiled=T...]
    psum x1 -> x0, blocking collectives: 40.5 us -> none  [per_device(): grad_point = lax.psum(local_grad, ('gx', 'gy')) * norm_scale]
  transfers between devices with their start and end apart: 6 -> 2, of which waited for: 4 -> 2; matrix products, arithmetic and copies ran while one was open for 10% -> 6% of each run, Pallas kernels for 0% -> 0%
where the time goes in v1:
time: 489 us; the launch traced here: 480 us
  Pallas kernels  262 us (54%)
  waiting for transfers between devices  74.3 us (15%)
  blocking collectives  69 us (14%)
  local copies, waits for them, and re-layouts  32.7 us (7%)
  other arithmetic  27.1 us (6%)
  between operations  14.4 us (3%)
    pallas_call x1, Pallas kernels, hidden_of(): pl.pallas_call(hidden_kernel, grid=(rows_here // SUB,), out_shape=(jax.Sh...  86.2 us
    all_gather x2, waiting for transfers between devices, spread(): return lax.all_gather(share, ('gx', 'gy'), axis=1, tiled=True)  74.2 us
    pallas_call x2, Pallas kernels, forward_local(): pl.pallas_call(forward_kernel, grid=(channels,), out_shape=jax.ShapeDtype...  71.2 us
    all_to_all x2, blocking collectives, own_sums(): lax.all_to_all(chunks, ('gx', 'gy'), split_axis=0, concat_axis=0, tiled=T...  69 us
    pallas_call x1, Pallas kernels, grad_of(): pl.pallas_call(grad_kernel, grid=(rows_here // SUB,), out_shape=jax.Shape...  62.1 us
    pallas_call x2, Pallas kernels, rows_of(): pl.pallas_call(rows_kernel, grid=(channels,), out_shape=jax.ShapeDtypeStr...  42.8 us
  transfers between devices with their start and end apart: 2, of which 2 were waited for; matrix products, arithmetic and copies ran while one was open for 6% of the time, Pallas kernels for 0%

profile of v1, /device:TPU:0, one launch (start us, length us, event | category | flops | bytes accessed | tf_op | source)
XLA Modules:
  0.0 480.0 jit_solution(2136705727881494488)
XLA Ops:
  7.2 0.0 all-gather.3.cloned.1.call-start
  7.2 1.1 fusion.33
  8.3 0.1 subtract_convert_fusion.3
  8.5 0.1 fusion.35
  8.6 1.1 fusion.31
  9.8 0.7 pad_maximum_fusion.6.table_y_ref
  10.5 0.8 pad_maximum_fusion.2.table_x_ref
  11.4 35.6 %forward_modes.2 = f32[32,64,128]{2,1,0:T(8,128)} custom-call(bf16[32,1024,512]{2,1,0:T(8,128)(2,1)} %act_ref.1, bf16[512,256]{1,0:T(8,128)(2,1)} %pad_maximum_fusion.6.table_y_ref, bf16[256,1024]{1,0:T(8,128)(2,1)} %pad_maximum_fusion.2.table_x_ref), custom_call_target="tpu_custom_call" | custom-call | tf_op jit(solution)/shard_map/forward_modes/pallas_call | solution.py:83
  47.0 1.3 broadcast_multiply_fusion.3
  48.3 1.2 mul.246
  49.5 1.6 copy.71
  51.1 1.8 reshape_reshape.3
  52.9 0.6 copy.12
  53.5 0.0 copy-start.2
  53.5 34.6 %all_to_all.10 = f32[32,64,128]{2,1,0:T(8,128)S(1)} all-to-all(f32[32,64,128]{2,1,0:T(8,128)S(1)} %copy.12), channel_id=1, replica_groups=mesh['gx'=4,'gy'=8] {'gx','gy'}, dimensions={0} | all-to-all | bytes 2097152 | tf_op jit(solution)/shard_map/all_to_all | solution.py:225
  88.1 0.1 reduce_sum.18
  88.2 0.4 fusion.2
  88.6 0.6 pad_maximum_fusion.10
  89.3 0.0 all-gather.3.cloned.1.call-update
  89.3 0.2 all-gather.5.cloned.1.call-start
  89.5 0.1 copy.15
  89.6 3.7 broadcast_multiply_fusion
  93.3 8.4 %mul.260.mix_ref = bf16[512,512]{1,0:T(8,128)(2,1)} reshape(bf16[32,16,32,16]{3,2,1,0:T(8,128)(2,1)} %get-tuple-element.38) | data formatting | bytes 1048576 | tf_op jit(solution)/shard_map/jit(kron)/mul | solution.py:242
  101.7 0.5 fusion.36
  102.3 2.1 fusion.19
  104.4 0.2 subtract_convert_fusion
  104.6 0.1 fusion.24
  104.8 0.7 pad_maximum_fusion.8.table_ref
  105.5 0.9 pad_maximum_fusion.4.table_ref
  106.4 33.1 %all-gather.3.cloned.1.call-done = f32[64,4096]{1,0:T(8,128)} async-done(((f32[64,128]{1,0:T(8,128)}), f32[64,4096]{1,0:T(8,128)}) %all-gather.3.cloned.1.call-update) | async-done | bytes 1048592 | tf_op jit(solution)/shard_map/all_gather | solution.py:230
  139.5 2.1 slice_multiply_fusion.2
  141.6 0.4 mul.251
  142.0 0.1 neg.9
  142.1 1.5 mul.249
  143.6 2.0 maximum_maximum_fusion.modes_ref
  145.5 21.4 %synthesis_rows.2.rows_ref = bf16[32,1024,128]{2,1,0:T(8,128)(2,1)} custom-call(f32[32,128,128]{2,1,0:T(8,128)} %maximum_maximum_fusion.modes_ref, bf16[1024,256]{1,0:T(8,128)(2,1)} %pad_maximum_fusion.4.table_ref), custom_call_target="tpu_custom_call" | custom-call | tf_op jit(solution)/shard_map/synthesis_rows/pallas_call | solution.py:116
  166.9 86.2 %hidden.1 = (bf16[32,1024,512]{2,1,0:T(8,128)(2,1)}, f32[32,32]{1,0:T(8,128)}) custom-call(bf16[32,1024,512]{2,1,0:T(8,128)(2,1)} %act_ref.1, bf16[32,1024,512]{2,1,0:T(8,128)(2,1)} %cot_ref.1, bf16[32,1024,128]{2,1,0:T(8,128)(2,1)} %synthesis_rows.2.rows_ref, bf16[512,512]{1,0:T(8,128)(2,1)} %mul.260.mix_ref, bf16[256,512]{1,0:T(8,128)(2,1)} %pad_maximum_fusion.8.table_ref), custom_call_target="tpu_custom_call" | custom-call | tf_op jit(solution)/shard_map/hidden/pallas_call | solution.py:195
  253.1 0.7 pad_bitcast_fusion
  253.8 35.6 %forward_modes.3 = f32[32,64,128]{2,1,0:T(8,128)} custom-call(bf16[32,1024,512]{2,1,0:T(8,128)(2,1)} %get-tuple-element.5.values_ref.hidden_ref, bf16[512,256]{1,0:T(8,128)(2,1)} %pad_maximum_fusion.6.table_y_ref, bf16[256,1024]{1,0:T(8,128)(2,1)} %pad_maximum_fusion.2.table_x_ref), custom_call_target="tpu_custom_call" | custom-call | tf_op jit(solution)/shard_map/forward_modes/pallas_call | solution.py:83
  289.4 1.3 broadcast_multiply_fusion.2
  290.7 1.2 mul.267
  291.9 1.6 copy.70
  293.5 1.8 concatenate.64
  295.3 0.1 maximum_bitcast_fusion
  295.4 0.6 copy.14
  296.0 0.0 copy-start.1
  296.1 34.4 %all_to_all.11 = f32[32,65,128]{2,1,0:T(8,128)S(1)} all-to-all(f32[32,65,128]{2,1,0:T(8,128)S(1)} %copy.14), channel_id=1, replica_groups=mesh['gx'=4,'gy'=8] {'gx','gy'}, dimensions={0} | all-to-all | bytes 2129920 | tf_op jit(solution)/shard_map/all_to_all | solution.py:225
  330.4 0.1 reduce_sum.19
  330.5 0.2 fusion.6
  330.7 0.6 pad_maximum_fusion.9
  331.4 0.0 all-gather.5.cloned.1.call-update
  331.4 8.4 %mul.275.mix_ref = bf16[512,512]{1,0:T(8,128)(2,1)} reshape(bf16[32,16,32,16]{3,2,1,0:T(8,128)(2,1)} %get-tuple-element.37) | data formatting | bytes 1048576 | tf_op jit(solution)/shard_map/jit(kron)/mul | solution.py:243
  339.8 0.1 multiply_add_fusion
  340.0 1.0 pad_maximum_fusion
  341.0 41.1 %all-gather.5.cloned.1.call-done = f32[65,4096]{1,0:T(8,128)} async-done(((f32[65,128]{1,0:T(8,128)}), f32[65,4096]{1,0:T(8,128)}) %all-gather.5.cloned.1.call-update) | async-done | bytes 1064976 | tf_op jit(solution)/shard_map/all_gather | solution.py:230
  382.1 0.9 slice.93
  383.0 0.6 slice_multiply_fusion.4
  383.6 2.1 slice_multiply_fusion
  385.7 0.4 mul.272
  386.1 0.1 neg.11
  386.3 1.5 mul.270
  387.7 1.9 maximum_maximum_fusion.1.modes_ref
  389.7 21.4 %synthesis_rows.3.rows_ref = bf16[32,1024,128]{2,1,0:T(8,128)(2,1)} custom-call(f32[32,128,128]{2,1,0:T(8,128)} %maximum_maximum_fusion.1.modes_ref, bf16[1024,256]{1,0:T(8,128)(2,1)} %pad_maximum_fusion.4.table_ref), custom_call_target="tpu_custom_call" | custom-call | tf_op jit(solution)/shard_map/synthesis_rows/pallas_call | solution.py:116
  411.1 62.1 %grad.1 = bf16[32,1024,512]{2,1,0:T(8,128)(2,1)} custom-call(bf16[32,1024,512]{2,1,0:T(8,128)(2,1)} %get-tuple-element.5.values_ref.hidden_ref, bf16[32,1024,128]{2,1,0:T(8,128)(2,1)} %synthesis_rows.3.rows_ref, bf16[512,512]{1,0:T(8,128)(2,1)} %mul.275.mix_ref, bf16[256,512]{1,0:T(8,128)(2,1)} %pad_maximum_fusion.8.table_ref), custom_call_target="tpu_custom_call" | custom-call | tf_op jit(solution)/shard_map/grad/pallas_call | solution.py:212
  (19 shorter events, 0.2 us)
Async XLA Ops:
  7.2 132.3 %all-gather.3.cloned.1.call-start = ((), (), s32[]{:S(2)}) async-start(), calls=%async_computation.2 | async-start | bytes 1081344 | tf_op jit(solution)/shard_map/all_gather | solution.py:230
  53.5 34.7 %copy-start = (bf16[2,32,32,128]{3,2,1,0:T(8,128)(2,1)S(1)}, bf16[2,32,32,128]{3,2,1,0:T(8,128)(2,1)}, u32[]{:S(2)}) copy-start(bf16[2,32,32,128]{3,2,1,0:T(8,128)(2,1)} %param.7) | copy-start | bytes 1572868
  53.5 36.0 %copy-start.2 = (bf16[32,32]{1,0:T(8,128)(2,1)S(1)}, bf16[32,32]{1,0:T(8,128)(2,1)}, u32[]{:S(2)}) copy-start(bf16[32,32]{1,0:T(8,128)(2,1)} %param.6) | copy-start | bytes 6148
  89.3 292.8 %all-gather.5.cloned.1.call-start = ((), (), s32[]{:S(2)}) async-start(), calls=%async_computation.3 | async-start | bytes 1216512 | tf_op jit(solution)/shard_map/all_gather | solution.py:230
  296.0 34.5 %copy-start.1 = (bf16[2,32,32,128]{3,2,1,0:T(8,128)(2,1)S(1)}, bf16[2,32,32,128]{3,2,1,0:T(8,128)(2,1)}, u32[]{:S(2)}) copy-start(bf16[2,32,32,128]{3,2,1,0:T(8,128)(2,1)} %param.7) | copy-start | bytes 1572868
Sparse Core Ops, SparseCore 0:
  89.4 50.0 all-gather.2
  331.5 50.5 all-gather.4
